TPU v7x, 512 devices: a whole 4x4x16 slice. The times are simulated.
512 devices in a mesh: task: 8 (over x_lo, y), shard: 64 (over z, x_hi, core).
Axes of the slice: x: 4 (x_hi: 2, x_lo: 2; x = x_hi * 2 + x_lo), y: 4, z: 16, core: 2. Of those that a mesh axis runs over, the one named last changes fastest.
Arguments:
- acts: bfloat16 [8, 1024, 4096], P('task', 'shard'), may hold values from -6 to 6
- cotangents: bfloat16 [8, 1024, 16384], P('task', 'shard'), may hold values from -0.75 to 0.75
- task_weights: bfloat16 [8, 4096, 16384], P('task', None, 'shard'), may hold values from -6 to 6
- example_count: int32 [8], P('task'), may hold values from 3 to 8, as said below
- example_start: int32 [8, 8], P('task'), may hold values from 0 to 1023, as said below
- example_len: int32 [8, 8], P('task'), may hold values from 1 to 128, as said below
Outputs:
- merged: bfloat16 [4096, 16384], P('task', 'shard')
Inputs may be any that keep to these rules, and one draw needn't show every extreme that they name: Task t's examples are counted in slots 0 to example_count[t] - 1; some task has 8. Slot e of every task lies in rows e * 128 to (e + 1) * 128 - 1: example_start[t, e] >= e * 128 and example_start[t, e] + example_len[t, e] <= (e + 1) * 128. `example_len`: every task has a counted slot of exactly 128 rows.
All inputs are finite; a program needn't handle non-finite values.
Results may differ from a plain program's by a relative error of at most 0.007.
Values may be sent and summed in bfloat16 or wider, within the bound.
A program may use at most 128 MiB of HBM per device.

v0:
```python
import jax
import jax.numpy as jnp
from jax import lax
from jax.sharding import Mesh
from jax.sharding import PartitionSpec as P

MOST = 128
SHARD = ("shard_0", "shard_1", "shard_2")


def in_order(pieces, dim):
    shape = list(pieces.shape[1:])
    shape[dim] *= pieces.shape[0]
    return jnp.moveaxis(pieces, 0, dim).reshape(shape)


def all_blocks(x, axes, order):
    pieces = x
    for k in order:
        pieces = lax.all_gather(pieces, axes[k])
    done = order[::-1]
    back = [done.index(k) for k in range(len(axes))]
    pieces = pieces.transpose(*back, *range(len(axes), pieces.ndim))
    return pieces.reshape(-1, *x.shape)


def whole_of(x, axes, order, dim):
    return in_order(all_blocks(x, axes, order), dim)


def per_device(acts, cotangents, task_weights, example_count, example_start, example_len):
    count = example_count[0]
    starts = example_start[0]
    lengths = example_len[0]
    weight_parts = lax.all_to_all(task_weights, "task", split_axis=1, concat_axis=0, tiled=True)
    rows = whole_of(acts[0], SHARD, (1, 0, 2), 0)
    grads = lax.all_to_all(cotangents[0], SHARD, split_axis=1, concat_axis=0, tiled=True)
    width = grads.shape[1]

    def one_slot(slot, total):
        block_x = lax.dynamic_slice_in_dim(rows, slot * MOST, MOST, 0)
        block_g = lax.dynamic_slice_in_dim(grads, slot * MOST, MOST, 0)
        position = slot * MOST + jnp.arange(MOST, dtype=jnp.int32)
        first = starts[slot]
        keep = (position >= first) & (position < first + lengths[slot]) & (slot < count)
        masked = jnp.where(keep[:, None], block_g, jnp.zeros_like(block_g))
        grad = lax.dot_general(
            block_x, masked, (((0,), (0,)), ((), ())), preferred_element_type=jnp.float32
        )
        return total + grad * grad

    empty = jnp.zeros((rows.shape[1], width), jnp.float32)
    total = lax.fori_loop(0, starts.shape[0], one_slot, empty)
    fisher = (total / count.astype(jnp.float32)).astype(jnp.bfloat16)
    fisher_parts = lax.all_to_all(fisher[None], "task", split_axis=1, concat_axis=0, tiled=True)
    weight_f = fisher_parts.astype(jnp.float32)
    numer = jnp.sum(weight_f * weight_parts.astype(jnp.float32), axis=0)
    denom = jnp.sum(weight_f, axis=0) + 1e-06
    return (numer / denom).astype(jnp.bfloat16)


def solution(mesh):
    split = Mesh(
        mesh.devices.reshape(mesh.shape["task"], 16, 2, 2),
        ("task", "shard_0", "shard_1", "shard_2"),
    )
    in_specs = (
        P("task", SHARD, None),
        P("task", SHARD, None),
        P("task", None, SHARD),
        P("task"),
        P("task", None),
        P("task", None),
    )
    out_specs = P("task", SHARD)
    return jax.shard_map(
        per_device, mesh=split, in_specs=in_specs, out_specs=out_specs, check_vma=False
    )
```

profile of v0, /device:TPU:1, one launch (start us, length us, event | category | flops | bytes accessed | tf_op | source)
XLA Modules:
  0.0 349.4 jit_solution(308229513936267923)
XLA Ops:
  6.5 8.5 %all_gather.15 = bf16[2,16,4096]{2,1,0:T(8,128)(2,1)} all-gather(bf16[1,16,4096]{2,1,0:T(8,128)(2,1)} %param.8), channel_id=1, replica_groups=mesh['task'=8,'shard_0'=16,'shard_1'=2,'shard_2'=2] {'shard_1'}, dimensions={0}, use_global_device_ids=true | all-gather | bytes 393216 | tf_op jit(solution)/shard_map/all_gather | solution.py:20
  15.2 73.9 %all-gather.5.cloned.1.call-done = bf16[32,16,4096]{2,1,0:T(8,128)(2,1)} async-done(((bf16[2,16,4096]{2,1,0:T(8,128)(2,1)}), bf16[32,16,4096]{2,1,0:T(8,128)(2,1)}) %all-gather.5.cloned.1.call-update) | async-done | bytes 4194320 | tf_op jit(solution)/shard_map/all_gather | solution.py:20
  89.2 1.1 copy.15
  90.4 19.7 %all-to-all-start = ((bf16[16,64,256]{2,0,1:T(8,128)(2,1)}), bf16[16,64,256]{2,0,1:T(8,128)(2,1)S(1)}, u32[]{:S(2)}, u32[]{:S(2)}) async-start(bf16[16,64,256]{2,0,1:T(8,128)(2,1)} %copy.15), calls=%async_computation | async-start | bytes 1048576 | tf_op jit(solution)/shard_map/all_to_all | solution.py:37
  110.7 25.1 %copy.23 = bf16[1,4096,256]{2,0,1:T(2,128)(2,1)} copy(bf16[1,4096,256]{2,1,0:T(8,128)(2,1)S(1)} %copy-done) | data formatting | bytes 4194304 | tf_op args[2]
  136.4 21.6 %reduce.1 = bf16[4096,256]{1,0:T(8,128)(2,1)S(1)} reduce(bf16[4096,1,256]{2,1,0:T(2,128)(2,1)} %bitcast.36, bf16[]{:T(256)} %broadcast.42), dimensions={1}, to_apply=%bitcast.27.reduce_sub_computation | reduce | bytes 4194306
  158.0 3.2 reshape.28
  161.2 7.7 %copy.14 = bf16[16,2,2,16,4096]{4,3,2,1,0:T(8,128)(2,1)} copy(bf16[16,2,2,16,4096]{4,3,1,0,2:T(8,128)(2,1)} %bitcast.41) | data formatting | bytes 16777216 | tf_op jit(solution)/shard_map/transpose | solution.py:23
  168.9 4.2 %all-to-all-start.2 = ((bf16[8,2,65536]{2,1,0:T(2,128)(2,1)}), bf16[8,2,65536]{2,1,0:T(2,128)(2,1)S(1)}, u32[]{:S(2)}, u32[]{:S(2)}) async-start(bf16[8,2,65536]{2,1,0:T(2,128)(2,1)} %reshape.28), calls=%async_computation.2 | async-start | bytes 4194304 | tf_op jit(solution)/shard_map/all_to_all | solution.py:35
  173.1 71.1 %while.14 = (s32[]{:T(128)}, f32[4096,256]{1,0:T(8,128)}, bf16[1024,4096]{1,0:T(8,128)(2,1)}, s32[8]{0:T(128)S(1)}, s32[8]{0:T(128)S(1)}, /*index=5*/s32[]{:T(12...) while((s32[]{:T(128)}, f32[4096,256]{1,0:T(8,128)}, ...), condition=%wide.region_1.2_spmd.clone, body=%wide.region_0.1_spmd.clone.sunk | while | flops 271614592 | bytes 9505118 | solution.py:53
  173.1 0.7 dynamic_slice.44
  176.9 3.9 %fusion.16 = f32[4096,256]{1,0:T(8,128)} fusion(f32[4096,256]{1,0:T(8,128)} %get-tuple-element.225, pred[]{:T(512)S(6)} %compare.3, bf16[1024,4096]{1,0:T(8,128)(2,1)} %get-tuple-element.237, s32[]{:T(128)S(6)} %select_n.29, bf16[1024,256]{1,0:T(8,128)(2,1)S(1)} %get-tuple-element.241, pred[128]{0:T(512)(128)(4,1)S(1)} %and_and_fusion.2), kind=kOutput, calls=%fused_computation.1.clone.1 | convolution fusion | flops 271613952 | bytes 9504768 | tf_op jit(solution)/shard_map/while/body/eval_jaxpr/dot_general | solution.py:47
  184.7 5.2 %fusion.16 = f32[4096,256]{1,0:T(8,128)} fusion(f32[4096,256]{1,0:T(8,128)} %get-tuple-element.225, pred[]{:T(512)S(6)} %compare.3, bf16[1024,4096]{1,0:T(8,128)(2,1)} %get-tuple-element.237, s32[]{:T(128)S(6)} %select_n.29, bf16[1024,256]{1,0:T(8,128)(2,1)S(1)} %get-tuple-element.241, pred[128]{0:T(512)(128)(4,1)S(1)} %and_and_fusion.2), kind=kOutput, calls=%fused_computation.1.clone.1 | convolution fusion | flops 271613952 | bytes 9504768 | tf_op jit(solution)/shard_map/while/body/eval_jaxpr/dot_general | solution.py:47
  189.9 0.6 dynamic_slice.44
  193.7 5.2 %fusion.16 = f32[4096,256]{1,0:T(8,128)} fusion(f32[4096,256]{1,0:T(8,128)} %get-tuple-element.225, pred[]{:T(512)S(6)} %compare.3, bf16[1024,4096]{1,0:T(8,128)(2,1)} %get-tuple-element.237, s32[]{:T(128)S(6)} %select_n.29, bf16[1024,256]{1,0:T(8,128)(2,1)S(1)} %get-tuple-element.241, pred[128]{0:T(512)(128)(4,1)S(1)} %and_and_fusion.2), kind=kOutput, calls=%fused_computation.1.clone.1 | convolution fusion | flops 271613952 | bytes 9504768 | tf_op jit(solution)/shard_map/while/body/eval_jaxpr/dot_general | solution.py:47
  199.0 0.6 dynamic_slice.44
  202.8 5.2 %fusion.16 = f32[4096,256]{1,0:T(8,128)} fusion(f32[4096,256]{1,0:T(8,128)} %get-tuple-element.225, pred[]{:T(512)S(6)} %compare.3, bf16[1024,4096]{1,0:T(8,128)(2,1)} %get-tuple-element.237, s32[]{:T(128)S(6)} %select_n.29, bf16[1024,256]{1,0:T(8,128)(2,1)S(1)} %get-tuple-element.241, pred[128]{0:T(512)(128)(4,1)S(1)} %and_and_fusion.2), kind=kOutput, calls=%fused_computation.1.clone.1 | convolution fusion | flops 271613952 | bytes 9504768 | tf_op jit(solution)/shard_map/while/body/eval_jaxpr/dot_general | solution.py:47
  211.8 5.2 %fusion.16 = f32[4096,256]{1,0:T(8,128)} fusion(f32[4096,256]{1,0:T(8,128)} %get-tuple-element.225, pred[]{:T(512)S(6)} %compare.3, bf16[1024,4096]{1,0:T(8,128)(2,1)} %get-tuple-element.237, s32[]{:T(128)S(6)} %select_n.29, bf16[1024,256]{1,0:T(8,128)(2,1)S(1)} %get-tuple-element.241, pred[128]{0:T(512)(128)(4,1)S(1)} %and_and_fusion.2), kind=kOutput, calls=%fused_computation.1.clone.1 | convolution fusion | flops 271613952 | bytes 9504768 | tf_op jit(solution)/shard_map/while/body/eval_jaxpr/dot_general | solution.py:47
  220.9 5.2 %fusion.16 = f32[4096,256]{1,0:T(8,128)} fusion(f32[4096,256]{1,0:T(8,128)} %get-tuple-element.225, pred[]{:T(512)S(6)} %compare.3, bf16[1024,4096]{1,0:T(8,128)(2,1)} %get-tuple-element.237, s32[]{:T(128)S(6)} %select_n.29, bf16[1024,256]{1,0:T(8,128)(2,1)S(1)} %get-tuple-element.241, pred[128]{0:T(512)(128)(4,1)S(1)} %and_and_fusion.2), kind=kOutput, calls=%fused_computation.1.clone.1 | convolution fusion | flops 271613952 | bytes 9504768 | tf_op jit(solution)/shard_map/while/body/eval_jaxpr/dot_general | solution.py:47
  229.9 5.2 %fusion.16 = f32[4096,256]{1,0:T(8,128)} fusion(f32[4096,256]{1,0:T(8,128)} %get-tuple-element.225, pred[]{:T(512)S(6)} %compare.3, bf16[1024,4096]{1,0:T(8,128)(2,1)} %get-tuple-element.237, s32[]{:T(128)S(6)} %select_n.29, bf16[1024,256]{1,0:T(8,128)(2,1)S(1)} %get-tuple-element.241, pred[128]{0:T(512)(128)(4,1)S(1)} %and_and_fusion.2), kind=kOutput, calls=%fused_computation.1.clone.1 | convolution fusion | flops 271613952 | bytes 9504768 | tf_op jit(solution)/shard_map/while/body/eval_jaxpr/dot_general | solution.py:47
  238.9 5.2 %fusion.16 = f32[4096,256]{1,0:T(8,128)} fusion(f32[4096,256]{1,0:T(8,128)} %get-tuple-element.225, pred[]{:T(512)S(6)} %compare.3, bf16[1024,4096]{1,0:T(8,128)(2,1)} %get-tuple-element.237, s32[]{:T(128)S(6)} %select_n.29, bf16[1024,256]{1,0:T(8,128)(2,1)S(1)} %get-tuple-element.241, pred[128]{0:T(512)(128)(4,1)S(1)} %and_and_fusion.2), kind=kOutput, calls=%fused_computation.1.clone.1 | convolution fusion | flops 271613952 | bytes 9504768 | tf_op jit(solution)/shard_map/while/body/eval_jaxpr/dot_general | solution.py:47
  244.2 2.5 fusion.9
  246.7 25.0 %copy.24 = bf16[1,4096,256]{2,0,1:T(2,128)(2,1)} copy(bf16[1,4096,256]{2,1,0:T(8,128)(2,1)S(1)} %fusion.9) | data formatting | bytes 4194304 | tf_op jit(solution)/shard_map/broadcast_in_dim | solution.py:55
  271.7 23.0 %reduce = bf16[4096,256]{1,0:T(8,128)(2,1)} reduce(bf16[4096,1,256]{2,1,0:T(2,128)(2,1)} %bitcast.37, bf16[]{:T(256)} %broadcast.42), dimensions={1}, to_apply=%bitcast.28.reduce_sub_computation | reduce | bytes 4194306
  294.7 5.8 %reshape.26 = bf16[8,2,65536]{2,1,0:T(2,128)(2,1)} reshape(bf16[4096,256]{1,0:T(8,128)(2,1)} %reduce) | data formatting | bytes 4194304
  300.5 5.1 %all-to-all-start.1 = ((bf16[8,2,65536]{2,1,0:T(2,128)(2,1)}), bf16[8,2,65536]{2,1,0:T(2,128)(2,1)}, u32[]{:S(2)}, u32[]{:S(2)}) async-start(bf16[8,2,65536]{2,1,0:T(2,128)(2,1)} %reshape.26), calls=%async_computation.1 | async-start | bytes 4194304 | tf_op jit(solution)/shard_map/all_to_all | solution.py:55
  305.7 4.4 %reshape.29 = bf16[4096,1,256]{2,1,0:T(2,128)(2,1)} reshape(bf16[8,2,65536]{2,1,0:T(2,128)(2,1)S(1)} %all-to-all-done.2) | data formatting | bytes 4194304
  310.0 2.5 copy.18
  312.6 19.4 %all-to-all-done.1 = bf16[8,2,65536]{2,1,0:T(2,128)(2,1)} async-done(((bf16[8,2,65536]{2,1,0:T(2,128)(2,1)}), bf16[8,2,65536]{2,1,0:T(2,128)(2,1)}, u32[]{:S(2)}, u32[]{:S(2)}) %all-to-all-start.1) | async-done | bytes 2097184 | tf_op jit(solution)/shard_map/all_to_all | solution.py:55
  332.0 6.7 %reshape.27 = bf16[4096,1,256]{2,1,0:T(2,128)(2,1)} reshape(bf16[8,2,65536]{2,1,0:T(2,128)(2,1)} %all-to-all-done.1) | data formatting | bytes 4194304
  338.7 2.5 copy.19
  341.8 0.8 divide_convert_fusion.1
  (40 shorter events, 14.5 us)
Async XLA Ops:
  6.5 82.6 %copy-start.1 = (bf16[1,16,16384]{2,1,0:T(8,128)(2,1)S(1)}, bf16[1,16,16384]{2,1,0:T(8,128)(2,1)}, u32[]{:S(2)}) copy-start(bf16[1,16,16384]{2,1,0:T(8,128)(2,1)} %param.9) | copy-start | bytes 1572868
  6.5 104.1 %copy-start = (bf16[1,4096,256]{2,1,0:T(8,128)(2,1)S(1)}, bf16[1,4096,256]{2,1,0:T(8,128)(2,1)}, u32[]{:S(2)}) copy-start(bf16[1,4096,256]{2,1,0:T(8,128)(2,1)} %param.10) | copy-start | bytes 6291460
  6.5 82.6 %all-gather.5.cloned.1.call-start = ((), (), s32[]{:S(2)}) async-start(), calls=%async_computation.3 | async-start | bytes 4456448 | tf_op jit(solution)/shard_map/all_gather | solution.py:20
  15.1 146.1 %all-gather.7.cloned.1.call-start = ((), (), s32[]{:S(2)}) async-start(), calls=%async_computation.4 | async-start | bytes 12582912 | tf_op jit(solution)/shard_map/all_gather | solution.py:20
  90.4 78.6 %all-to-all-start = ((bf16[16,64,256]{2,0,1:T(8,128)(2,1)}), bf16[16,64,256]{2,0,1:T(8,128)(2,1)S(1)}, u32[]{:S(2)}, u32[]{:S(2)}) async-start(bf16[16,64,256]{2,0,1:T(8,128)(2,1)} %copy.15), calls=%async_computation | async-start | bytes 1048576 | tf_op jit(solution)/shard_map/all_to_all | solution.py:37
  168.9 4.2 %copy-start.2 = (s32[1,8]{1,0:T(1,128)S(1)}, s32[1,8]{1,0:T(1,128)}, u32[]{:S(2)}) copy-start(s32[1,8]{1,0:T(1,128)} %param.12) | copy-start | bytes 100
  168.9 4.2 %copy-start.3 = (s32[1,8]{1,0:T(1,128)S(1)}, s32[1,8]{1,0:T(1,128)}, u32[]{:S(2)}) copy-start(s32[1,8]{1,0:T(1,128)} %param.13) | copy-start | bytes 100
  168.9 131.6 %all-to-all-start.2 = ((bf16[8,2,65536]{2,1,0:T(2,128)(2,1)}), bf16[8,2,65536]{2,1,0:T(2,128)(2,1)S(1)}, u32[]{:S(2)}, u32[]{:S(2)}) async-start(bf16[8,2,65536]{2,1,0:T(2,128)(2,1)} %reshape.28), calls=%async_computation.2 | async-start | bytes 4194304 | tf_op jit(solution)/shard_map/all_to_all | solution.py:35
  300.5 31.4 %all-to-all-start.1 = ((bf16[8,2,65536]{2,1,0:T(2,128)(2,1)}), bf16[8,2,65536]{2,1,0:T(2,128)(2,1)}, u32[]{:S(2)}, u32[]{:S(2)}) async-start(bf16[8,2,65536]{2,1,0:T(2,128)(2,1)} %reshape.26), calls=%async_computation.1 | async-start | bytes 4194304 | tf_op jit(solution)/shard_map/all_to_all | solution.py:55
Sparse Core Ops, SparseCore 0:
  15.2 73.8 all-gather.4
  91.2 36.9 all-gather.6
where the time goes:
time: 351 us; the launch traced here: 349 us
  local copies, waits for them, and re-layouts  94.8 us (27%)
  waiting for transfers between devices  93.4 us (27%)
  other arithmetic  53.5 us (15%)
  matrix products  40.6 us (12%)
  starting transfers between devices  29 us (8%)
  loops' own time  15.5 us (4%)
  between operations  14.1 us (4%)
  blocking collectives  8.54 us (2%)
    all_gather x2, waiting for transfers between devices, all_blocks(): pieces = lax.all_gather(pieces, axes[k])  73.9 us
    unnamed x16, local copies, waits for them, and re-layouts  48.4 us
    unnamed x3, other arithmetic  44.6 us
    dot_general x8, matrix products, one_slot(): lax.dot_general(block_x, masked, (((0,), (0,)), ((), ())), preferred_elem...  40.6 us
    broadcast_in_dim x1, local copies, waits for them, and re-layouts, per_device(): fisher[None]  25 us
    all_to_all x1, starting transfers between devices, per_device(): lax.all_to_all(cotangents[0], SHARD, split_axis=1, concat_axis=0, tiled=T...  19.7 us
    all_to_all x1, waiting for transfers between devices, per_device(): lax.all_to_all(fisher[None], 'task', split_axis=1, concat_axis=0, tiled=T...  19.4 us
    another operation x1, loops' own time, per_device(): total = lax.fori_loop(0, starts.shape[0], one_slot, empty)  15.5 us
  transfers between devices with their start and end apart: 5, of which 2 were waited for; matrix products, arithmetic and copies ran while one was open for 51% of the time, Pallas kernels for 0%

commit v1 on v0

v1 whole, which is shorter than its diff:
```python
import jax
import jax.numpy as jnp
from jax import lax
from jax.experimental import pallas as pl
from jax.experimental.pallas import tpu as pltpu
from jax.sharding import Mesh
from jax.sharding import PartitionSpec as P

XL, Y, Z, XH, C = 2, 4, 16, 2, 2
AXES = ("xl", "y", "z", "xh", "c")
EX = 8
MOST = 128
ROWS = 16
CHUNK = 256
NCH = 4
BLK = 256
DB = 512
TILE = 128
HALF = Z // 2


def kernel(count_ref, start_ref, len_ref, x_ref, g_ref, w_ref, o_ref,
           xs, gs, ws, fs, fr, mk,
           loc_sem, q_send, q_recv, r_send, r_recv,
           gz_send, gz_recv, gx_send, gx_recv, gc_send, gc_recv,
           w_send, w_recv, f_send, f_recv):
    xl, y, z, xh, c = (lax.axis_index(a) for a in AXES)
    task = xl * Y + y
    oxh, oc = 1 - xh, 1 - c
    quart = c * 2 + xh

    def zmod(v):
        return lax.rem(v + 2 * Z, Z)

    def remote(src, dst, ssem, rsem, **dev):
        return pltpu.make_async_remote_copy(
            src_ref=src, dst_ref=dst, send_sem=ssem, recv_sem=rsem,
            device_id=dev, device_id_type=pl.DeviceIdType.MESH)

    barrier = pltpu.get_barrier_semaphore()

    def tell(**dev):
        pl.semaphore_signal(barrier, inc=1, device_id=dev,
                            device_id_type=pl.DeviceIdType.MESH)

    tell(xh=xh, c=oc)
    tell(xh=oxh, c=c)
    tell(xh=oxh, c=oc)

    def tell_z(d, carry):
        tell(z=zmod(z + d))
        return carry
    lax.fori_loop(1, Z, tell_z, 0)

    def tell_t(k, carry):
        t2 = lax.rem(task + k, XL * Y)
        tell(xl=t2 // Y, y=lax.rem(t2, Y))
        return carry
    lax.fori_loop(1, XL * Y, tell_t, 0)

    src_q = task // 2
    src_c, src_xh = src_q // 2, lax.rem(src_q, 2)
    own_src = src_q == quart

    def tell_f(k, carry):
        t2 = lax.rem(task + k, XL * Y)
        tell(xl=t2 // Y, y=lax.rem(t2, Y), xh=src_xh, c=src_c)
        return carry
    lax.fori_loop(1, XL * Y, tell_f, 0)

    @pl.when(jnp.logical_not(own_src))
    def _():
        tell(xh=src_xh, c=src_c)

    me = xh * 2 + c

    def local_x(n):
        return pltpu.make_async_copy(
            x_ref.at[:, pl.ds(pl.multiple_of(quart * 1024 + n * CHUNK, 128), CHUNK)],
            xs.at[n, z, pl.ds(pl.multiple_of(me * ROWS, ROWS), ROWS), :], loc_sem.at[n])

    for n in range(NCH):
        local_x(n).start()
    own_g = g_ref.at[:, pl.ds(pl.multiple_of(z * 1024, 128), 1024)]
    local_g = pltpu.make_async_copy(own_g, gs.at[z, xh, c], loc_sem.at[4])
    local_g.start()
    local_w = pltpu.make_async_copy(
        w_ref.at[pl.ds(pl.multiple_of(task * DB, DB), DB), :], ws.at[task], loc_sem.at[5])
    local_w.start()

    position = lax.broadcasted_iota(jnp.int32, (MOST, 128), 0)
    for e in range(EX):
        first = start_ref[0, e] - e * MOST
        last = jnp.where(e < count_ref[0], first + len_ref[0, e], first)
        keep = jnp.where(position >= first, 1.0, 0.0) * jnp.where(position < last, 1.0, 0.0)
        mk[e] = keep.astype(jnp.bfloat16)

    pl.semaphore_wait(
        barrier, 3 + (Z - 1) + 2 * (XL * Y - 1) + 1 - own_src.astype(jnp.int32))

    def quad_copy(n, h, k):
        return remote(
            x_ref.at[:, pl.ds(pl.multiple_of((k * 2 + h) * 1024 + n * CHUNK, 128), CHUNK)],
            xs.at[n, z, pl.ds(pl.multiple_of(me * ROWS, ROWS), ROWS), :],
            q_send.at[n, h * 2 + k], q_recv.at[n, me], xh=h, c=k)

    def quad_arrival(n, h, k):
        return remote(
            x_ref.at[:, pl.ds(0, CHUNK)],
            xs.at[n, z, pl.ds(pl.multiple_of((h * 2 + k) * ROWS, ROWS), ROWS), :],
            q_send.at[n, me], q_recv.at[n, h * 2 + k], xh=h, c=k)

    others = ((oxh, c), (xh, oc), (oxh, oc))

    def order(m):
        return lax.rem(m // 2 + y, 2) * 2 + m % 2

    for m in range(NCH):
        for h, k in others:
            quad_copy(order(m), h, k).start()

    def gz_copy(zp):
        return remote(
            g_ref.at[:, pl.ds(pl.multiple_of(zp * 1024, 128), 1024)],
            gs.at[z, xh, c], gz_send.at[zp], gz_recv.at[z], z=zp)

    def gz_arrival(zp):
        return remote(own_g, gs.at[zp, xh, c], gz_send.at[z], gz_recv.at[zp], z=zp)

    gz_copy(zmod(z + HALF)).start()

    def far(i, carry):
        d = HALF - i
        gz_copy(zmod(z + d)).start()
        gz_copy(zmod(z - d)).start()
        return carry
    lax.fori_loop(1, HALF, far, 0)

    def w_copy(k):
        t2 = lax.rem(task + k, XL * Y)
        return remote(
            w_ref.at[pl.ds(pl.multiple_of(t2 * DB, DB), DB), :], ws.at[task],
            w_send.at[k], w_recv.at[k], xl=t2 // Y, y=lax.rem(t2, Y))

    def w_start(k, carry):
        w_copy(k).start()
        return carry
    lax.fori_loop(1, XL * Y, w_start, 0)

    def gx_copy(zp, src):
        return remote(src, gs.at[zp, xh, c], gx_send.at[zp], gx_recv.at[zp], xh=oxh)

    def gx_arrival(zp):
        return remote(own_g, gs.at[zp, oxh, c], gx_send.at[zp], gx_recv.at[zp], xh=oxh)

    def gc_copy(zp, h, src):
        return remote(src, gs.at[zp, h, c], gc_send.at[zp, h], gc_recv.at[zp, h], c=oc)

    def gc_arrival(zp, h):
        return remote(own_g, gs.at[zp, h, oc], gc_send.at[zp, h], gc_recv.at[zp, h], c=oc)

    def take_z(zp):
        gz_arrival(zp).wait_recv()
        gx_copy(zp, gs.at[zp, xh, c]).start()
        gc_copy(zp, xh, gs.at[zp, xh, c]).start()

    def take_x(zp):
        gx_arrival(zp).wait_recv()
        gc_copy(zp, oxh, gs.at[zp, oxh, c]).start()

    gx_copy(z, own_g).start()
    gc_copy(z, xh, own_g).start()

    def ring(way, s, m):
        n = order(m)
        step = 1 if way == 0 else -1
        held = zmod(z - step * (s - 1))
        return remote(xs.at[n, held], xs.at[n, held], r_send.at[way, m, s - 1],
                      r_recv.at[way, m, s - 1], z=zmod(z + step))

    def ring_arrival(way, s, m):
        n = order(m)
        step = 1 if way == 0 else -1
        came = zmod(z - step * s)
        return remote(xs.at[n, came], xs.at[n, came], r_send.at[way, m, s - 1],
                      r_recv.at[way, m, s - 1], z=zmod(z - step))

    for m in range(NCH):
        n = order(m)
        local_x(n).wait()
        for h, k in others:
            quad_arrival(n, h, k).wait_recv()
        ring(0, 1, m).start()
        ring(1, 1, m).start()

    def both(s, last):
        for m in range(NCH):
            for way in range(2):
                ring_arrival(way, s - 1, m).wait_recv()
                if not last or (m < 2) == (way == 0):
                    ring(way, s, m).start()

    both(2, False)
    take_x(z)

    def mid(s, carry):
        both(s, False)
        d = 11 - s
        take_z(zmod(z + d))

        @pl.when(d < HALF)
        def _():
            take_z(zmod(z - d))

        @pl.when(s > 3)
        def _():
            take_x(zmod(z + d + 1))

        @pl.when(s > 4)
        def _():
            take_x(zmod(z - d - 1))
        return carry
    lax.fori_loop(3, HALF, mid, 0)
    both(HALF, True)
    for d in (3, 2, 1):
        take_z(zmod(z + d))
        take_z(zmod(z - d))
        take_x(zmod(z + d + 1))
        take_x(zmod(z - d - 1))
    take_x(zmod(z + 1))
    take_x(zmod(z - 1))

    for m in range(NCH):
        ring_arrival(0 if m < 2 else 1, HALF, m).wait_recv()

    local_g.wait()

    def gc_wait(zp, carry):
        for h in range(2):
            gc_arrival(zp, h).wait_recv()
        return carry
    lax.fori_loop(0, Z, gc_wait, 0)

    inv = jnp.ones((1, BLK), jnp.float32) / jnp.full((1, BLK), count_ref[0].astype(jnp.float32))

    def tile_of(i):
        b = lax.rem(i // 4 + y, 2)
        return b, lax.rem(i, 4)

    def send_tile(i, act):
        b, r = tile_of(i)
        t2 = quart * 2 + b
        for f in range(4):
            h, k = f // 2, f % 2
            mine = jnp.logical_and(t2 == task, me == f)
            dst = fr.at[task, r]
            src = fs.at[i, f]

            @pl.when(jnp.logical_not(mine))
            def _():
                cp = remote(src, dst, f_send.at[i, f], f_recv.at[task, r],
                            xl=t2 // Y, y=lax.rem(t2, Y), xh=h, c=k)
                if act == "start":
                    cp.start()
                else:
                    cp.wait_send()

            @pl.when(mine)
            def _():
                if act == "start":
                    pltpu.make_async_copy(src, dst, f_recv.at[task, r]).start()

    def compute(i):
        b, r = tile_of(i)
        n = b * 2 + r // 2
        col = pl.multiple_of(lax.rem(r, 2) * TILE, TILE)
        xts = []
        for e in range(EX):
            xe = xs[n, 2 * e:2 * e + 2, :, pl.ds(col, TILE)].reshape(MOST, TILE) * mk[e]
            xts.append(xe.T)
        for f in range(4):
            total = jnp.zeros((TILE, BLK), jnp.float32)
            for e in range(EX):
                ge = gs[2 * e:2 * e + 2, :, :, :, f * BLK:(f + 1) * BLK].reshape(MOST, BLK)
                grad = jnp.dot(xts[e], ge, preferred_element_type=jnp.float32)
                total = total + grad * grad
            fs[i, f] = (total * inv).astype(jnp.bfloat16)

    def tile_step(i, carry):
        compute(i)

        @pl.when(i > 0)
        def _():
            send_tile(i - 1, "start")
        return carry
    lax.fori_loop(0, 8, tile_step, 0)
    send_tile(7, "start")

    local_w.wait()

    def w_wait(k, carry):
        w_copy(k).wait()
        return carry
    lax.fori_loop(1, XL * Y, w_wait, 0)

    def merge(r, carry):
        for t2 in range(XL * Y):
            pltpu.make_async_copy(fs.at[0, 0], fr.at[t2, r], f_recv.at[t2, r]).wait()
        rows = pl.ds(pl.multiple_of(r * TILE, TILE), TILE)
        numer = jnp.zeros((TILE, BLK), jnp.float32)
        denom = jnp.zeros((TILE, BLK), jnp.float32)
        for t2 in range(XL * Y):
            f32 = fr[t2, r].astype(jnp.float32)
            numer = numer + f32 * ws[t2, rows, :].astype(jnp.float32)
            denom = denom + f32
        o_ref[rows, :] = (numer / (denom + 1e-6)).astype(jnp.bfloat16)
        return carry
    lax.fori_loop(0, 4, merge, 0)

    for m in range(NCH):
        for h, k in others:
            quad_copy(order(m), h, k).wait_send()

    def z_out(d, carry):
        gz_copy(zmod(z + d)).wait_send()
        return carry
    lax.fori_loop(1, Z, z_out, 0)

    def q_out(zp, carry):
        gx_copy(zp, own_g).wait_send()
        gc_copy(zp, 0, own_g).wait_send()
        gc_copy(zp, 1, own_g).wait_send()
        return carry
    lax.fori_loop(0, Z, q_out, 0)

    def r_out(s, carry):
        for m in range(NCH):
            for way in range(2):
                ring(way, s, m).wait_send()
        return carry
    lax.fori_loop(1, HALF, r_out, 0)
    for m in range(NCH):
        ring(0 if m < 2 else 1, HALF, m).wait_send()

    def f_out(i, carry):
        send_tile(i, "wait")
        return carry
    lax.fori_loop(0, 8, f_out, 0)


def per_device(acts, cotangents, task_weights, example_count, example_start, example_len):
    dma = pltpu.SemaphoreType.DMA
    vmem = pltpu.VMEM
    bf = jnp.bfloat16
    return pl.pallas_call(
        kernel,
        out_shape=jax.ShapeDtypeStruct((DB, BLK), bf),
        in_specs=[pl.BlockSpec(memory_space=pltpu.SMEM)] * 3
        + [pl.BlockSpec(memory_space=pl.ANY)] * 3,
        out_specs=pl.BlockSpec(memory_space=pltpu.VMEM),
        scratch_shapes=[
            vmem((NCH, Z, 64, CHUNK), bf),
            vmem((Z, 2, 2, ROWS, 1024), bf),
            vmem((8, DB, BLK), bf),
            vmem((8, 4, TILE, BLK), bf),
            vmem((8, 4, TILE, BLK), bf),
            vmem((EX, MOST, 128), bf),
            dma((6,)),
            dma((NCH, 4)), dma((NCH, 4)),
            dma((2, NCH, HALF)), dma((2, NCH, HALF)),
            dma((Z,)), dma((Z,)),
            dma((Z,)), dma((Z,)),
            dma((Z, 2)), dma((Z, 2)),
            dma((8,)), dma((8,)),
            dma((8, 4)), dma((8, 4)),
        ],
        compiler_params=pltpu.CompilerParams(
            collective_id=0, has_side_effects=True, vmem_limit_bytes=40 << 20),
        name="merge",
    )(example_count, example_start, example_len,
      acts[0], cotangents[0], task_weights[0])


def solution(mesh):
    split = Mesh(mesh.devices.reshape(XL, Y, Z, XH, C), AXES)
    task, shard = ("xl", "y"), ("z", "xh", "c")
    in_specs = (
        P(task, shard, None),
        P(task, shard, None),
        P(task, None, shard),
        P(task),
        P(task, None),
        P(task, None),
    )
    return jax.shard_map(
        per_device, mesh=split, in_specs=in_specs, out_specs=P(task, shard), check_vma=False)
```

time: 351 us -> 116 us (0.33)
  Pallas kernels: 0 us -> 110 us
  waiting for transfers between devices: 93.4 us -> 0 us
  local copies, waits for them, and re-layouts: 94.8 us -> 5.54 us
  other arithmetic: 53.5 us -> 0 us
  matrix products: 40.6 us -> 0 us
  starting transfers between devices: 29 us -> 0 us
  loops' own time: 15.5 us -> 0 us
  between operations: 14.1 us -> 0.67 us
  blocking collectives: 8.54 us -> 0 us
    pallas_call x0 -> x1, Pallas kernels: none -> 110 us  [per_device(): pl.pallas_call(kernel, out_shape=jax.ShapeDtypeStruct((DB, BLK), bf), in_...]
    all_gather x2 -> x0, waiting for transfers between devices: 73.9 us -> none  [all_blocks(): pieces = lax.all_gather(pieces, axes[k])]
    unnamed x3 -> x0, other arithmetic: 44.6 us -> none
    unnamed x16 -> x11, local copies, waits for them, and re-layouts: 48.4 us -> 5.54 us
    dot_general x8 -> x0, matrix products: 40.6 us -> none  [one_slot(): lax.dot_general(block_x, masked, (((0,), (0,)), ((), ())), preferred_elem...]
    all_to_all x3 -> x0, starting transfers between devices: 29 us -> none  [the longest x1 19.7 us: per_device(): lax.all_to_all(cotangents[0], SHARD, split_axis=1, concat_axis=0, tiled=T...]
    broadcast_in_dim x1 -> x0, local copies, waits for them, and re-layouts: 25 us -> none  [per_device(): fisher[None]]
    all_to_all x3 -> x0, waiting for transfers between devices: 19.4 us -> none  [the longest x1 19.4 us: per_device(): lax.all_to_all(fisher[None], 'task', split_axis=1, concat_axis=0, tiled=T...]
  transfers between devices with their start and end apart: 5 -> 0, of which waited for: 2 -> 0; matrix products, arithmetic and copies ran while one was open for 51% -> 0% of each run, Pallas kernels for 0% -> 0%
where the time goes in v1:
time: 116 us
  Pallas kernels  110 us (95%)
  local copies, waits for them, and re-layouts  5.54 us (5%)
    pallas_call x1, Pallas kernels, per_device(): pl.pallas_call(kernel, out_shape=jax.ShapeDtypeStruct((DB, BLK), bf), in_...  110 us
    unnamed x11, local copies, waits for them, and re-layouts  5.54 us

profile of v1, /device:TPU:1, one launch (start us, length us, event | category | flops | bytes accessed | tf_op | source)
XLA Modules:
  0.0 115.8 jit_solution(9459489645154072984)
XLA Ops:
  0.7 0.0 copy-start
  0.7 1.6 %copy-done = bf16[1,4096,256]{2,1,0:T(8,128)(2,1)S(1)} copy-done((bf16[1,4096,256]{2,1,0:T(8,128)(2,1)S(1)}, bf16[1,4096,256]{2,1,0:T(8,128)(2,1)}, u32[]{:S(2)}) %copy-start) | copy-done | bytes 2097176
  2.2 0.0 copy-start.1
  2.2 1.0 copy-done.1
  3.3 0.0 copy-start.2
  3.3 0.9 copy-done.2
  4.2 0.0 copy-start.3
  4.2 0.7 copy-done.3
  4.8 0.0 copy-start.4
  4.8 0.7 copy-done.4
  5.5 109.6 %merge.1 = bf16[512,256]{1,0:T(8,128)(2,1)S(1)} custom-call(s32[1]{0:T(128)S(6)} %copy.8.count_ref, s32[1,8]{1,0:T(1,128)S(1)} %copy-done.3, s32[1,8]{1,0:T(1,128)S(1)} %copy-done.4, bf16[16,4096]{1,0:T(8,128)(2,1)S(1)} %bitcast.5, bf16[16,16384]{1,0:T(8,128)(2,1)S(1)} %bitcast.4, bf16[4096,256]{1,0:T(8,128)(2,1)S(1)} %bitcast.3), custom_call_target="tpu_custom_call" | custom-call | tf_op jit(solution)/shard_map/merge/pallas_call | solution.py:355
  115.1 0.7 copy.9
Async XLA Ops:
  0.7 1.6 %copy-start = (bf16[1,4096,256]{2,1,0:T(8,128)(2,1)S(1)}, bf16[1,4096,256]{2,1,0:T(8,128)(2,1)}, u32[]{:S(2)}) copy-start(bf16[1,4096,256]{2,1,0:T(8,128)(2,1)} %param.8) | copy-start | bytes 6291460
  2.2 1.0 copy-start.1
  3.3 0.9 copy-start.2
  4.2 0.7 copy-start.3
  4.8 0.7 copy-start.4

commit v2 on v1

--- a/solution.py
+++ b/solution.py
@@ -17,12 +17,14 @@
 DB = 512
 TILE = 128
 HALF = Z // 2
-
-
-def kernel(count_ref, start_ref, len_ref, x_ref, g_ref, w_ref, o_ref,
-           xs, gs, ws, fs, fr, mk,
-           loc_sem, q_send, q_recv, r_send, r_recv,
-           gz_send, gz_recv, gx_send, gx_recv, gc_send, gc_recv,
+START = (1, 3, 5, 7)
+FIRST = 11
+
+
+def kernel(count_hbm, start_hbm, len_hbm, x_ref, g_ref, w_ref, o_ref,
+           xs, gs, ws, fs, fr, mk, count_ref, start_ref, len_ref,
+           cr, loc_sem, q_send, q_recv, r_send, r_recv,
+           cz_send, cz_recv, gx_send, gx_recv, gc_send, gc_recv,
            w_send, w_recv, f_send, f_recv):
     xl, y, z, xh, c = (lax.axis_index(a) for a in AXES)
     task = xl * Y + y
@@ -47,10 +49,8 @@
     tell(xh=oxh, c=c)
     tell(xh=oxh, c=oc)
 
-    def tell_z(d, carry):
-        tell(z=zmod(z + d))
-        return carry
-    lax.fori_loop(1, Z, tell_z, 0)
+    tell(z=zmod(z + 1))
+    tell(z=zmod(z - 1))
 
     def tell_t(k, carry):
         t2 = lax.rem(task + k, XL * Y)
@@ -88,6 +88,13 @@
         w_ref.at[pl.ds(pl.multiple_of(task * DB, DB), DB), :], ws.at[task], loc_sem.at[5])
     local_w.start()
 
+    tables = [pltpu.make_async_copy(a, b, loc_sem.at[6 + i]) for i, (a, b) in enumerate(
+        ((count_hbm, count_ref), (start_hbm, start_ref), (len_hbm, len_ref)))]
+    for copy in tables:
+        copy.start()
+    for copy in tables:
+        copy.wait()
+
     position = lax.broadcasted_iota(jnp.int32, (MOST, 128), 0)
     for e in range(EX):
         first = start_ref[0, e] - e * MOST
@@ -96,7 +103,7 @@
         mk[e] = keep.astype(jnp.bfloat16)
 
     pl.semaphore_wait(
-        barrier, 3 + (Z - 1) + 2 * (XL * Y - 1) + 1 - own_src.astype(jnp.int32))
+        barrier, 3 + 2 + 2 * (XL * Y - 1) + 1 - own_src.astype(jnp.int32))
 
     def quad_copy(n, h, k):
         return remote(
@@ -119,33 +126,78 @@
         for h, k in others:
             quad_copy(order(m), h, k).start()
 
-    def gz_copy(zp):
+    def cols(way, dist, base):
+        width = 512 if dist == HALF else 1024
+        off = 512 if dist == HALF and way == 1 else 0
+        return pl.ds(pl.multiple_of(base + off, 128), width)
+
+    def cz(way, s, r, src, dst):
+        return remote(src, dst, cz_send.at[way, s - 1, r], cz_recv.at[way, s - 1, r],
+                      z=zmod(z + (1 if way == 0 else -1)))
+
+    def cz_arrival(way, s, r, far):
+        dst = cr.at[way, 0, 0, :, cols(way, HALF if far else 0, 0)]
+        cz(way, s, r, dst, dst).wait_recv()
+
+    def cz_first(way, r):
+        far = r + 1 == HALF
+        dest = zmod(z + (r + 1) * (1 if way == 0 else -1))
+        src = g_ref.at[:, cols(way, r + 1, dest * 1024)]
+        if r == 0:
+            dst = gs.at[z, xh, c]
+        else:
+            dst = cr.at[way, 0, r - 1, :, cols(way, r + 1, 0)]
+        cz(way, 1, r, src, dst).start()
+
+    def cz_pass(way, s, r, far, final):
+        cz_arrival(way, s - 1, r + 1, far)
+        dist = HALF if far else 0
+        src = cr.at[way, s - 2, r, :, cols(way, dist, 0)]
+        if final:
+            origin = zmod(z - (s - 1) * (1 if way == 0 else -1))
+            dst = gs.at[origin, xh, c, :, cols(way, dist, 0)]
+        else:
+            dst = cr.at[way, s - 1, r - 1, :, cols(way, dist, 0)]
+        cz(way, s, r, src, dst).start()
+
+    def cz_step(s):
+        @pl.when(s < HALF)
+        def _():
+            for way in range(2):
+                cz_pass(way, s, HALF - s, True, False)
+
+            def middle(j, carry):
+                for way in range(2):
+                    cz_pass(way, s, HALF - 1 - s - j, False, False)
+                return carry
+            lax.fori_loop(0, HALF - 1 - s, middle, 0)
+            for way in range(2):
+                cz_pass(way, s, 0, False, True)
+
+        @pl.when(s == HALF)
+        def _():
+            for way in range(2):
+                cz_pass(way, s, 0, True, True)
+
+    def cz_wait_send(way, s, r, far):
+        src = cr.at[way, 0, 0, :, cols(way, HALF if far else 0, 0)]
+        cz(way, s, r, src, src).wait_send()
+
+    def w_copy(k, piece=None):
+        t2 = lax.rem(task + k, XL * Y)
+        if piece is None:
+            base, rows, span = t2 * DB, pl.ds(0, DB), DB
+        else:
+            base, rows, span = t2 * DB + piece * 64, pl.ds(pl.multiple_of(piece * 64, 64), 64), 64
         return remote(
-            g_ref.at[:, pl.ds(pl.multiple_of(zp * 1024, 128), 1024)],
-            gs.at[z, xh, c], gz_send.at[zp], gz_recv.at[z], z=zp)
-
-    def gz_arrival(zp):
-        return remote(own_g, gs.at[zp, xh, c], gz_send.at[z], gz_recv.at[zp], z=zp)
-
-    gz_copy(zmod(z + HALF)).start()
-
-    def far(i, carry):
-        d = HALF - i
-        gz_copy(zmod(z + d)).start()
-        gz_copy(zmod(z - d)).start()
-        return carry
-    lax.fori_loop(1, HALF, far, 0)
-
-    def w_copy(k):
-        t2 = lax.rem(task + k, XL * Y)
-        return remote(
-            w_ref.at[pl.ds(pl.multiple_of(t2 * DB, DB), DB), :], ws.at[task],
+            w_ref.at[pl.ds(pl.multiple_of(base, 64), span), :], ws.at[task, rows, :],
             w_send.at[k], w_recv.at[k], xl=t2 // Y, y=lax.rem(t2, Y))
 
-    def w_start(k, carry):
-        w_copy(k).start()
-        return carry
-    lax.fori_loop(1, XL * Y, w_start, 0)
+    def w_some(piece):
+        def one(k, carry):
+            w_copy(k, piece).start()
+            return carry
+        lax.fori_loop(1, XL * Y, one, 0)
 
     def gx_copy(zp, src):
         return remote(src, gs.at[zp, xh, c], gx_send.at[zp], gx_recv.at[zp], xh=oxh)
@@ -159,10 +211,22 @@
     def gc_arrival(zp, h):
         return remote(own_g, gs.at[zp, h, oc], gc_send.at[zp, h], gc_recv.at[zp, h], c=oc)
 
-    def take_z(zp):
-        gz_arrival(zp).wait_recv()
+    def pass_on(zp):
         gx_copy(zp, gs.at[zp, xh, c]).start()
         gc_copy(zp, xh, gs.at[zp, xh, c]).start()
+
+    def take_z(s):
+        @pl.when(s < HALF)
+        def _():
+            for way in range(2):
+                cz_arrival(way, s, 0, False)
+                pass_on(zmod(z - s * (1 if way == 0 else -1)))
+
+        @pl.when(s == HALF)
+        def _():
+            for way in range(2):
+                cz_arrival(way, s, 0, True)
+            pass_on(zmod(z + HALF))
 
     def take_x(zp):
         gx_arrival(zp).wait_recv()
@@ -170,6 +234,10 @@
 
     gx_copy(z, own_g).start()
     gc_copy(z, xh, own_g).start()
+
+    for r in range(HALF - 1, -1, -1):
+        for way in range(2):
+            cz_first(way, r)
 
     def ring(way, s, m):
         n = order(m)
@@ -185,54 +253,59 @@
         return remote(xs.at[n, came], xs.at[n, came], r_send.at[way, m, s - 1],
                       r_recv.at[way, m, s - 1], z=zmod(z - step))
 
-    for m in range(NCH):
-        n = order(m)
-        local_x(n).wait()
-        for h, k in others:
-            quad_arrival(n, h, k).wait_recv()
-        ring(0, 1, m).start()
-        ring(1, 1, m).start()
-
-    def both(s, last):
+    def ring_part(slot, m):
+        s = slot - START[m]
+
+        @pl.when(s == 1)
+        def _():
+            n = order(m)
+            local_x(n).wait()
+            for h, k in others:
+                quad_arrival(n, h, k).wait_recv()
+
+        for way in range(2):
+            turns = HALF if (m < 2) == (way == 0) else HALF - 1
+
+            @pl.when(jnp.logical_and(s >= 2, s <= turns + 1))
+            def _():
+                ring_arrival(way, s - 1, m).wait_recv()
+
+            @pl.when(jnp.logical_and(s >= 1, s <= turns))
+            def _():
+                ring(way, s, m).start()
+
+    def take_pair(d, fn):
+        fn(zmod(z + d))
+
+        @pl.when(d < HALF)
+        def _():
+            fn(zmod(z - d))
+
+    def early(slot, carry):
+        @pl.when(jnp.logical_and(slot >= 2, slot <= HALF))
+        def _():
+            cz_step(slot)
         for m in range(NCH):
-            for way in range(2):
-                ring_arrival(way, s - 1, m).wait_recv()
-                if not last or (m < 2) == (way == 0):
-                    ring(way, s, m).start()
-
-    both(2, False)
-    take_x(z)
-
-    def mid(s, carry):
-        both(s, False)
-        d = 11 - s
-        take_z(zmod(z + d))
-
-        @pl.when(d < HALF)
-        def _():
-            take_z(zmod(z - d))
-
-        @pl.when(s > 3)
-        def _():
-            take_x(zmod(z + d + 1))
-
-        @pl.when(s > 4)
-        def _():
-            take_x(zmod(z - d - 1))
-        return carry
-    lax.fori_loop(3, HALF, mid, 0)
-    both(HALF, True)
-    for d in (3, 2, 1):
-        take_z(zmod(z + d))
-        take_z(zmod(z - d))
-        take_x(zmod(z + d + 1))
-        take_x(zmod(z - d - 1))
-    take_x(zmod(z + 1))
-    take_x(zmod(z - 1))
-
-    for m in range(NCH):
-        ring_arrival(0 if m < 2 else 1, HALF, m).wait_recv()
-
+            ring_part(slot, m)
+
+        @pl.when(jnp.logical_and(slot >= 2, slot <= HALF + 1))
+        def _():
+            take_z(slot - 1)
+
+        @pl.when(jnp.logical_and(slot >= 3, slot <= HALF + 2))
+        def _():
+            take_pair(slot - 2, take_x)
+
+        @pl.when(slot == 1)
+        def _():
+            take_x(z)
+
+        @pl.when(slot <= 8)
+        def _():
+            w_some(slot - 1)
+        return carry
+
+    lax.fori_loop(1, FIRST, early, 0)
     local_g.wait()
 
     def gc_wait(zp, carry):
@@ -247,28 +320,27 @@
         b = lax.rem(i // 4 + y, 2)
         return b, lax.rem(i, 4)
 
-    def send_tile(i, act):
+    def send_part(i, f, act):
         b, r = tile_of(i)
         t2 = quart * 2 + b
-        for f in range(4):
-            h, k = f // 2, f % 2
-            mine = jnp.logical_and(t2 == task, me == f)
-            dst = fr.at[task, r]
-            src = fs.at[i, f]
-
-            @pl.when(jnp.logical_not(mine))
-            def _():
-                cp = remote(src, dst, f_send.at[i, f], f_recv.at[task, r],
-                            xl=t2 // Y, y=lax.rem(t2, Y), xh=h, c=k)
-                if act == "start":
-                    cp.start()
-                else:
-                    cp.wait_send()
-
+        h, k = f // 2, f % 2
+        mine = jnp.logical_and(t2 == task, me == f)
+        dst = fr.at[task, r]
+        src = fs.at[i, f]
+
+        @pl.when(jnp.logical_not(mine))
+        def _():
+            cp = remote(src, dst, f_send.at[i, f], f_recv.at[task, r],
+                        xl=t2 // Y, y=lax.rem(t2, Y), xh=h, c=k)
+            if act == "start":
+                cp.start()
+            else:
+                cp.wait_send()
+
+        if act == "start":
             @pl.when(mine)
             def _():
-                if act == "start":
-                    pltpu.make_async_copy(src, dst, f_recv.at[task, r]).start()
+                pltpu.make_async_copy(src, dst, f_recv.at[task, r]).start()
 
     def compute(i):
         b, r = tile_of(i)
@@ -285,16 +357,20 @@
                 grad = jnp.dot(xts[e], ge, preferred_element_type=jnp.float32)
                 total = total + grad * grad
             fs[i, f] = (total * inv).astype(jnp.bfloat16)
+            if f > 0:
+                send_part(i, f - 1, "start")
 
     def tile_step(i, carry):
+        for m in range(NCH):
+            ring_part(i + FIRST, m)
+
+        @pl.when(i > 0)
+        def _():
+            send_part(i - 1, 3, "start")
         compute(i)
-
-        @pl.when(i > 0)
-        def _():
-            send_tile(i - 1, "start")
         return carry
     lax.fori_loop(0, 8, tile_step, 0)
-    send_tile(7, "start")
+    send_part(7, 3, "start")
 
     local_w.wait()
 
@@ -321,10 +397,16 @@
         for h, k in others:
             quad_copy(order(m), h, k).wait_send()
 
-    def z_out(d, carry):
-        gz_copy(zmod(z + d)).wait_send()
-        return carry
-    lax.fori_loop(1, Z, z_out, 0)
+    def c_out(s, carry):
+        for way in range(2):
+            cz_wait_send(way, s, HALF - s, True)
+
+        def near(r, carry):
+            for way in range(2):
+                cz_wait_send(way, s, r, False)
+            return carry
+        return lax.fori_loop(0, HALF - s, near, carry)
+    lax.fori_loop(1, HALF + 1, c_out, 0)
 
     def q_out(zp, carry):
         gx_copy(zp, own_g).wait_send()
@@ -343,7 +425,8 @@
         ring(0 if m < 2 else 1, HALF, m).wait_send()
 
     def f_out(i, carry):
-        send_tile(i, "wait")
+        for f in range(4):
+            send_part(i, f, "wait")
         return carry
     lax.fori_loop(0, 8, f_out, 0)
 
@@ -355,8 +438,7 @@
     return pl.pallas_call(
         kernel,
         out_shape=jax.ShapeDtypeStruct((DB, BLK), bf),
-        in_specs=[pl.BlockSpec(memory_space=pltpu.SMEM)] * 3
-        + [pl.BlockSpec(memory_space=pl.ANY)] * 3,
+        in_specs=[pl.BlockSpec(memory_space=pl.ANY)] * 6,
         out_specs=pl.BlockSpec(memory_space=pltpu.VMEM),
         scratch_shapes=[
             vmem((NCH, Z, 64, CHUNK), bf),
@@ -365,17 +447,19 @@
             vmem((8, 4, TILE, BLK), bf),
             vmem((8, 4, TILE, BLK), bf),
             vmem((EX, MOST, 128), bf),
-            dma((6,)),
+            pltpu.SMEM((1,), jnp.int32), pltpu.SMEM((1, EX), jnp.int32),
+            pltpu.SMEM((1, EX), jnp.int32),
+            vmem((2, HALF - 1, HALF - 1, ROWS, 1024), bf), dma((9,)),
             dma((NCH, 4)), dma((NCH, 4)),
             dma((2, NCH, HALF)), dma((2, NCH, HALF)),
-            dma((Z,)), dma((Z,)),
+            dma((2, HALF, HALF)), dma((2, HALF, HALF)),
             dma((Z,)), dma((Z,)),
             dma((Z, 2)), dma((Z, 2)),
             dma((8,)), dma((8,)),
             dma((8, 4)), dma((8, 4)),
         ],
         compiler_params=pltpu.CompilerParams(
-            collective_id=0, has_side_effects=True, vmem_limit_bytes=40 << 20),
+            collective_id=0, has_side_effects=True, vmem_limit_bytes=67_000_000),
         name="merge",
     )(example_count, example_start, example_len,
       acts[0], cotangents[0], task_weights[0])

time: 116 us -> 96.7 us (0.83)
  Pallas kernels: 110 us -> 94.2 us
  local copies, waits for them, and re-layouts: 5.54 us -> 1.67 us
    pallas_call x1, Pallas kernels: 110 us -> 94.2 us  [per_device(): pl.pallas_call(kernel, out_shape=jax.ShapeDtypeStruct((DB, BLK), bf), in_...]
    unnamed x11 -> x1, local copies, waits for them, and re-layouts: 5.54 us -> 1.67 us
where the time goes in v2:
time: 96.7 us; the launch traced here: 96.6 us
  Pallas kernels  94.2 us (97%)
  local copies, waits for them, and re-layouts  1.67 us (2%)
    pallas_call x1, Pallas kernels, per_device(): pl.pallas_call(kernel, out_shape=jax.ShapeDtypeStruct((DB, BLK), bf), in_...  94.2 us

profile of v2, /device:TPU:1, one launch (start us, length us, event | category | flops | bytes accessed | tf_op | source)
XLA Modules:
  0.0 96.6 jit_solution(1690759412717598357)
XLA Ops:
  0.7 94.2 %merge.1 = bf16[512,256]{1,0:T(8,128)(2,1)} custom-call(s32[1]{0:T(128)S(6)} %copy.8.count_hbm, s32[1,8]{1,0:T(1,128)} %start_hbm.1, s32[1,8]{1,0:T(1,128)} %len_hbm.1, bf16[16,4096]{1,0:T(8,128)(2,1)} %bitcast.5, bf16[16,16384]{1,0:T(8,128)(2,1)} %bitcast.4, bf16[4096,256]{1,0:T(8,128)(2,1)} %bitcast.3), custom_call_target="tpu_custom_call" | custom-call | tf_op jit(solution)/shard_map/merge/pallas_call | solution.py:438
  94.9 1.7 %copy.9 = bf16[512,256]{1,0:T(8,128)(2,1)} copy(bf16[512,256]{1,0:T(8,128)(2,1)} %merge.1) | data formatting | bytes 524288

commit v3 on v2

--- a/solution.py
+++ b/solution.py
@@ -18,7 +18,8 @@
 TILE = 128
 HALF = Z // 2
 START = (1, 3, 5, 7)
-FIRST = 11
+FIRST = 10
+PIECES = (1, 1, 1, 1, 1, 1, 1, 1)
 
 
 def kernel(count_hbm, start_hbm, len_hbm, x_ref, g_ref, w_ref, o_ref,
@@ -120,7 +121,7 @@
     others = ((oxh, c), (xh, oc), (oxh, oc))
 
     def order(m):
-        return lax.rem(m // 2 + y, 2) * 2 + m % 2
+        return lax.rem(m + y, 2) * 2 + m // 2
 
     for m in range(NCH):
         for h, k in others:
@@ -206,10 +207,11 @@
         return remote(own_g, gs.at[zp, oxh, c], gx_send.at[zp], gx_recv.at[zp], xh=oxh)
 
     def gc_copy(zp, h, src):
-        return remote(src, gs.at[zp, h, c], gc_send.at[zp, h], gc_recv.at[zp, h], c=oc)
-
-    def gc_arrival(zp, h):
-        return remote(own_g, gs.at[zp, h, oc], gc_send.at[zp, h], gc_recv.at[zp, h], c=oc)
+        return remote(src, gs.at[zp, h, c], gc_send.at[zp, h], gc_recv.at[0], c=oc)
+
+    def gc_all():
+        whole = gs.at[:, :, oc]
+        pltpu.make_async_copy(whole, whole, gc_recv.at[0]).wait()
 
     def pass_on(zp):
         gx_copy(zp, gs.at[zp, xh, c]).start()
@@ -285,40 +287,44 @@
         @pl.when(jnp.logical_and(slot >= 2, slot <= HALF))
         def _():
             cz_step(slot)
+
+        @pl.when(slot >= 2)
+        def _():
+            take_z(slot - 1)
+
+        @pl.when(slot >= 4)
+        def _():
+            take_pair(slot - 3, take_x)
+
+        @pl.when(slot == 2)
+        def _():
+            take_x(z)
         for m in range(NCH):
             ring_part(slot, m)
-
-        @pl.when(jnp.logical_and(slot >= 2, slot <= HALF + 1))
-        def _():
-            take_z(slot - 1)
-
-        @pl.when(jnp.logical_and(slot >= 3, slot <= HALF + 2))
-        def _():
-            take_pair(slot - 2, take_x)
-
-        @pl.when(slot == 1)
-        def _():
-            take_x(z)
-
-        @pl.when(slot <= 8)
-        def _():
-            w_some(slot - 1)
-        return carry
-
+        sent = 0
+        for at, n in enumerate(PIECES):
+            if n:
+                @pl.when(slot == at)
+                def _(lo=sent, hi=sent + n):
+                    for piece in range(lo, hi):
+                        w_some(piece)
+            sent += n
+        return carry
+
+    for piece in range(PIECES[0]):
+        w_some(piece)
     lax.fori_loop(1, FIRST, early, 0)
+    take_pair(FIRST - 3, take_x)
+    take_pair(FIRST - 2, take_x)
     local_g.wait()
 
-    def gc_wait(zp, carry):
-        for h in range(2):
-            gc_arrival(zp, h).wait_recv()
-        return carry
-    lax.fori_loop(0, Z, gc_wait, 0)
+    gc_all()
 
     inv = jnp.ones((1, BLK), jnp.float32) / jnp.full((1, BLK), count_ref[0].astype(jnp.float32))
 
     def tile_of(i):
-        b = lax.rem(i // 4 + y, 2)
-        return b, lax.rem(i, 4)
+        b = lax.rem(i // 2 + y, 2)
+        return b, (i // 4) * 2 + lax.rem(i, 2)
 
     def send_part(i, f, act):
         b, r = tile_of(i)
@@ -379,6 +385,43 @@
         return carry
     lax.fori_loop(1, XL * Y, w_wait, 0)
 
+    for m in range(NCH):
+        for h, k in others:
+            quad_copy(order(m), h, k).wait_send()
+
+    def c_out(s, carry):
+        for way in range(2):
+            cz_wait_send(way, s, HALF - s, True)
+
+        def near(r, carry):
+            for way in range(2):
+                cz_wait_send(way, s, r, False)
+            return carry
+        return lax.fori_loop(0, HALF - s, near, carry)
+    lax.fori_loop(1, HALF + 1, c_out, 0)
+
+    def q_out(zp, carry):
+        gx_copy(zp, own_g).wait_send()
+        gc_copy(zp, 0, own_g).wait_send()
+        gc_copy(zp, 1, own_g).wait_send()
+        return carry
+    lax.fori_loop(0, Z, q_out, 0)
+
+    def r_out(s, carry):
+        for m in range(NCH):
+            for way in range(2):
+                ring(way, s, m).wait_send()
+        return carry
+    lax.fori_loop(1, HALF, r_out, 0)
+    for m in range(NCH):
+        ring(0 if m < 2 else 1, HALF, m).wait_send()
+
+    def f_out(i, carry):
+        for f in range(4):
+            send_part(i, f, "wait")
+        return carry
+    lax.fori_loop(0, 8, f_out, 0)
+
     def merge(r, carry):
         for t2 in range(XL * Y):
             pltpu.make_async_copy(fs.at[0, 0], fr.at[t2, r], f_recv.at[t2, r]).wait()
@@ -392,43 +435,6 @@
         o_ref[rows, :] = (numer / (denom + 1e-6)).astype(jnp.bfloat16)
         return carry
     lax.fori_loop(0, 4, merge, 0)
-
-    for m in range(NCH):
-        for h, k in others:
-            quad_copy(order(m), h, k).wait_send()
-
-    def c_out(s, carry):
-        for way in range(2):
-            cz_wait_send(way, s, HALF - s, True)
-
-        def near(r, carry):
-            for way in range(2):
-                cz_wait_send(way, s, r, False)
-            return carry
-        return lax.fori_loop(0, HALF - s, near, carry)
-    lax.fori_loop(1, HALF + 1, c_out, 0)
-
-    def q_out(zp, carry):
-        gx_copy(zp, own_g).wait_send()
-        gc_copy(zp, 0, own_g).wait_send()
-        gc_copy(zp, 1, own_g).wait_send()
-        return carry
-    lax.fori_loop(0, Z, q_out, 0)
-
-    def r_out(s, carry):
-        for m in range(NCH):
-            for way in range(2):
-                ring(way, s, m).wait_send()
-        return carry
-    lax.fori_loop(1, HALF, r_out, 0)
-    for m in range(NCH):
-        ring(0 if m < 2 else 1, HALF, m).wait_send()
-
-    def f_out(i, carry):
-        for f in range(4):
-            send_part(i, f, "wait")
-        return carry
-    lax.fori_loop(0, 8, f_out, 0)
 
 
 def per_device(acts, cotangents, task_weights, example_count, example_start, example_len):
@@ -454,7 +460,7 @@
             dma((2, NCH, HALF)), dma((2, NCH, HALF)),
             dma((2, HALF, HALF)), dma((2, HALF, HALF)),
             dma((Z,)), dma((Z,)),
-            dma((Z, 2)), dma((Z, 2)),
+            dma((Z, 2)), dma((1,)),
             dma((8,)), dma((8,)),
             dma((8, 4)), dma((8, 4)),
         ],

time: 96.7 us -> 93 us (0.962)
  Pallas kernels: 94.2 us -> 90.5 us
    pallas_call x1, Pallas kernels: 94.2 us -> 90.5 us  [per_device(): pl.pallas_call(kernel, out_shape=jax.ShapeDtypeStruct((DB, BLK), bf), in_...]
where the time goes in v3:
time: 93 us; the launch traced here: 92.8 us
  Pallas kernels  90.5 us (97%)
  local copies, waits for them, and re-layouts  1.67 us (2%)
    pallas_call x1, Pallas kernels, per_device(): pl.pallas_call(kernel, out_shape=jax.ShapeDtypeStruct((DB, BLK), bf), in_...  90.5 us

profile of v3, /device:TPU:1, one launch (start us, length us, event | category | flops | bytes accessed | tf_op | source)
XLA Modules:
  0.0 92.8 jit_solution(17148569885553333862)
XLA Ops:
  0.7 90.5 %merge.1 = bf16[512,256]{1,0:T(8,128)(2,1)} custom-call(s32[1]{0:T(128)S(6)} %copy.8.count_hbm, s32[1,8]{1,0:T(1,128)} %start_hbm.1, s32[1,8]{1,0:T(1,128)} %len_hbm.1, bf16[16,4096]{1,0:T(8,128)(2,1)} %bitcast.5, bf16[16,16384]{1,0:T(8,128)(2,1)} %bitcast.4, bf16[4096,256]{1,0:T(8,128)(2,1)} %bitcast.3), custom_call_target="tpu_custom_call" | custom-call | tf_op jit(solution)/shard_map/merge/pallas_call | solution.py:444
  91.2 1.7 %copy.9 = bf16[512,256]{1,0:T(8,128)(2,1)} copy(bf16[512,256]{1,0:T(8,128)(2,1)} %merge.1) | data formatting | bytes 524288

commit v4 on v3

--- a/solution.py
+++ b/solution.py
@@ -17,14 +17,15 @@
 DB = 512
 TILE = 128
 HALF = Z // 2
-START = (1, 3, 5, 7)
+START = (1, 3, 5, 6)
+DIRECT = 7
 FIRST = 10
 PIECES = (1, 1, 1, 1, 1, 1, 1, 1)
 
 
 def kernel(count_hbm, start_hbm, len_hbm, x_ref, g_ref, w_ref, o_ref,
            xs, gs, ws, fs, fr, mk, count_ref, start_ref, len_ref,
-           cr, loc_sem, q_send, q_recv, r_send, r_recv,
+           cr, ov, loc_sem, q_send, q_recv, r_send, r_recv,
            cz_send, cz_recv, gx_send, gx_recv, gc_send, gc_recv,
            w_send, w_recv, f_send, f_recv):
     xl, y, z, xh, c = (lax.axis_index(a) for a in AXES)
@@ -122,10 +123,6 @@
 
     def order(m):
         return lax.rem(m + y, 2) * 2 + m // 2
-
-    for m in range(NCH):
-        for h, k in others:
-            quad_copy(order(m), h, k).start()
 
     def cols(way, dist, base):
         width = 512 if dist == HALF else 1024
@@ -222,24 +219,41 @@
         def _():
             for way in range(2):
                 cz_arrival(way, s, 0, False)
-                pass_on(zmod(z - s * (1 if way == 0 else -1)))
+                zp = zmod(z - s * (1 if way == 0 else -1))
+                pass_on(zp)
+
+                @pl.when(s >= DIRECT)
+                def _(zp=zp):
+                    diagonal(zp)
 
         @pl.when(s == HALF)
         def _():
             for way in range(2):
                 cz_arrival(way, s, 0, True)
             pass_on(zmod(z + HALF))
+            diagonal(zmod(z + HALF))
 
     def take_x(zp):
         gx_arrival(zp).wait_recv()
         gc_copy(zp, oxh, gs.at[zp, oxh, c]).start()
 
-    gx_copy(z, own_g).start()
-    gc_copy(z, xh, own_g).start()
+    def take_x_last(zp):
+        gx_arrival(zp).wait_recv()
+
+    def diagonal(zp):
+        block = gs.at[zp, xh, c]
+        remote(block, block, gc_send.at[zp, oxh], gc_recv.at[0], xh=oxh, c=oc).start()
 
     for r in range(HALF - 1, -1, -1):
         for way in range(2):
             cz_first(way, r)
+
+    for m in range(NCH):
+        for h, k in others:
+            quad_copy(order(m), h, k).start()
+
+    gx_copy(z, own_g).start()
+    gc_copy(z, xh, own_g).start()
 
     def ring(way, s, m):
         n = order(m)
@@ -314,8 +328,8 @@
     for piece in range(PIECES[0]):
         w_some(piece)
     lax.fori_loop(1, FIRST, early, 0)
-    take_pair(FIRST - 3, take_x)
-    take_pair(FIRST - 2, take_x)
+    take_pair(FIRST - 3, take_x_last)
+    take_pair(FIRST - 2, take_x_last)
     local_g.wait()
 
     gc_all()
@@ -432,9 +446,16 @@
             f32 = fr[t2, r].astype(jnp.float32)
             numer = numer + f32 * ws[t2, rows, :].astype(jnp.float32)
             denom = denom + f32
-        o_ref[rows, :] = (numer / (denom + 1e-6)).astype(jnp.bfloat16)
+        ov[rows, :] = (numer / (denom + 1e-6)).astype(jnp.bfloat16)
+        pltpu.make_async_copy(ov.at[rows, :], o_ref.at[rows, :], loc_sem.at[r]).start()
         return carry
     lax.fori_loop(0, 4, merge, 0)
+
+    def leave(r, carry):
+        rows = pl.ds(pl.multiple_of(r * TILE, TILE), TILE)
+        pltpu.make_async_copy(ov.at[rows, :], o_ref.at[rows, :], loc_sem.at[r]).wait()
+        return carry
+    lax.fori_loop(0, 4, leave, 0)
 
 
 def per_device(acts, cotangents, task_weights, example_count, example_start, example_len):
@@ -445,7 +466,7 @@
         kernel,
         out_shape=jax.ShapeDtypeStruct((DB, BLK), bf),
         in_specs=[pl.BlockSpec(memory_space=pl.ANY)] * 6,
-        out_specs=pl.BlockSpec(memory_space=pltpu.VMEM),
+        out_specs=pl.BlockSpec(memory_space=pl.ANY),
         scratch_shapes=[
             vmem((NCH, Z, 64, CHUNK), bf),
             vmem((Z, 2, 2, ROWS, 1024), bf),
@@ -455,7 +476,7 @@
             vmem((EX, MOST, 128), bf),
             pltpu.SMEM((1,), jnp.int32), pltpu.SMEM((1, EX), jnp.int32),
             pltpu.SMEM((1, EX), jnp.int32),
-            vmem((2, HALF - 1, HALF - 1, ROWS, 1024), bf), dma((9,)),
+            vmem((2, HALF - 1, HALF - 1, ROWS, 1024), bf), vmem((DB, BLK), bf), dma((9,)),
             dma((NCH, 4)), dma((NCH, 4)),
             dma((2, NCH, HALF)), dma((2, NCH, HALF)),
             dma((2, HALF, HALF)), dma((2, HALF, HALF)),

time: 93 us -> 92.9 us (level)
  no operation moved by 1% of the time
where the time goes in v4:
time: 92.9 us; the launch traced here: 92.8 us
  Pallas kernels  90.4 us (97%)
  local copies, waits for them, and re-layouts  1.67 us (2%)
    pallas_call x1, Pallas kernels, per_device(): pl.pallas_call(kernel, out_shape=jax.ShapeDtypeStruct((DB, BLK), bf), in_...  90.4 us

profile of v4, /device:TPU:1, one launch (start us, length us, event | category | flops | bytes accessed | tf_op | source)
XLA Modules:
  0.0 92.8 jit_solution(13133951491817626359)
XLA Ops:
  0.7 90.4 %merge.1 = bf16[512,256]{1,0:T(8,128)(2,1)} custom-call(s32[1]{0:T(128)S(6)} %copy.8.count_hbm, s32[1,8]{1,0:T(1,128)} %start_hbm.1, s32[1,8]{1,0:T(1,128)} %len_hbm.1, bf16[16,4096]{1,0:T(8,128)(2,1)} %bitcast.5, bf16[16,16384]{1,0:T(8,128)(2,1)} %bitcast.4, bf16[4096,256]{1,0:T(8,128)(2,1)} %bitcast.3), custom_call_target="tpu_custom_call" | custom-call | tf_op jit(solution)/shard_map/merge/pallas_call | solution.py:465
  91.1 1.7 %copy.9 = bf16[512,256]{1,0:T(8,128)(2,1)} copy(bf16[512,256]{1,0:T(8,128)(2,1)} %merge.1) | data formatting | bytes 524288
